TPU v7x, 128 devices: a whole 4x4x4 slice. The times are simulated.
128 devices in a mesh: gr: 16 (over y_hi, z, core), gc: 8 (over x, y_lo).
Axes of the slice: x: 4, y: 4 (y_hi: 2, y_lo: 2; y = y_hi * 2 + y_lo), z: 4, core: 2. Of those that a mesh axis runs over, the one named last changes fastest.
Arguments:
- shards: bfloat16 [16, 8, 56, 18432], P('gr', 'gc'), may hold values from -4.5 to 4.5, as said below
- counts: int32 [8, 16], replicated, may hold values from 1 to 56, 448 in all within a row
Outputs:
- next_shards: float32 [16, 8, 56, 18432], P('gr', 'gc')
Inputs may be any that keep to these rules, and one draw needn't show every extreme that they name: Each row of counts sums to 448: the devices (0, c) to (15, c) together hold row block c of the iterate, in order of g. `shards`: rows of a buffer at or beyond its device's count are not part of the iterate and hold arbitrary values.
All inputs are finite; a program needn't handle non-finite values.
Results may differ from a plain program's by a relative error of at most 0.0003.
Values may be sent and summed in bfloat16 or wider, within the bound.
A program may use at most 128 MiB of HBM per device.

v0:
```python
import jax
import jax.numpy as jnp
from jax import lax
from jax.sharding import PartitionSpec as P

M = 3584
N = 18432
linear_coef = 3.4445
cubic_coef = -4.775
quintic_coef = 2.0315
highest = lax.Precision.HIGHEST


def rows_against(left_rows, right_rows):
    return lax.dot_general(
        left_rows, right_rows, (((1,), (1,)), ((), ())), preferred_element_type=jnp.float32
    )


def make_accumulate(panel, sub_width, running, segment):
    seg_width = segment.shape[1]

    def one_turn(turn_index, summed):
        seg_part = lax.dynamic_slice_in_dim(segment, turn_index * sub_width, sub_width, 1)
        panel_rows = lax.dynamic_slice_in_dim(panel, turn_index * sub_width, sub_width, 0).astype(
            jnp.float32
        )
        return summed + jnp.dot(
            seg_part, panel_rows, precision=highest, preferred_element_type=jnp.float32
        )

    return lax.fori_loop(0, seg_width // sub_width, one_turn, running)


def body(shards, counts):
    own_rows = shards[0, 0]
    grid_rows = lax.axis_size("gr")
    grid_cols = lax.axis_size("gc")
    row_block = lax.axis_index("gc")
    capacity = own_rows.shape[0]
    full_width = own_rows.shape[1]
    col_width = full_width // grid_rows
    block_rows = M // grid_cols
    gram_width = M // grid_rows
    my_counts = lax.dynamic_index_in_dim(counts, row_block, 0, keepdims=False)
    my_starts = jnp.cumsum(my_counts) - my_counts
    received = lax.all_to_all(own_rows, "gr", split_axis=1, concat_axis=0, tiled=True)
    position = jnp.arange(block_rows, dtype=jnp.int32)
    holder = jnp.sum((my_starts[None, :] <= position[:, None]).astype(jnp.int32), axis=1) - 1
    one_hot = holder[:, None] == jnp.arange(grid_rows, dtype=jnp.int32)[None, :]
    first_row = jnp.sum(jnp.where(one_hot, my_starts[None, :], 0), axis=1)
    source_rows = holder * capacity + position - first_row
    own_block = jnp.take(received, source_rows, axis=0)
    panel = lax.all_gather(own_block, "gc", axis=0, tiled=True)
    partial_value = rows_against(own_block, panel)
    gram_block = lax.psum_scatter(partial_value, "gr", scatter_dimension=1, tiled=True) / N
    gram_cols = lax.all_gather(gram_block, "gc", axis=0, tiled=True)
    square_part = lax.dot_general(
        gram_block,
        gram_cols,
        (((1,), (1,)), ((), ())),
        precision=highest,
        preferred_element_type=jnp.float32,
    )
    square_block = lax.psum_scatter(square_part, "gr", scatter_dimension=1, tiled=True)
    poly_block = cubic_coef * gram_block + quintic_coef * square_block
    start_sum = jnp.zeros((block_rows, col_width), jnp.float32)
    product = make_accumulate(
        panel, gram_width, start_sum, lax.all_gather(poly_block, "gr", axis=1, tiled=True)
    )
    update_block = linear_coef * own_block.astype(jnp.float32) + product
    slot_ids = jnp.arange(capacity, dtype=jnp.int32)
    target_rows = jnp.minimum(my_starts[:, None] + slot_ids[None, :], block_rows - 1).reshape(-1)
    is_live = (slot_ids[None, :] < my_counts[:, None]).reshape(-1)
    outgoing = jnp.where(
        is_live[:, None], jnp.take(update_block, target_rows, axis=0), jnp.zeros((), jnp.float32)
    )
    returned = lax.all_to_all(outgoing, "gr", split_axis=0, concat_axis=1, tiled=True)
    return returned.reshape(1, 1, capacity, full_width)


def solution(mesh):
    placed = (P("gr", "gc", None, None), P())
    return jax.shard_map(
        body, mesh=mesh, in_specs=placed, out_specs=P("gr", "gc", None, None), check_vma=False
    )
```

profile of v0, /device:TPU:1, one launch (start us, length us, event | category | flops | bytes accessed | tf_op | source)
XLA Modules:
  0.0 709.8 jit_solution(17190910258514315236)
XLA Ops:
  6.5 1.8 copy.24
  8.4 1.7 copy.15
  10.1 9.5 %all-to-all-start = ((bf16[56,16,1152]{2,0,1:T(8,128)(2,1)}), bf16[56,16,1152]{2,0,1:T(8,128)(2,1)S(1)}, u32[]{:S(2)}, u32[]{:S(2)}) async-start(bf16[56,16,1152]{2,0,1:T(8,128)(2,1)} %copy.15), calls=%async_computation | async-start | bytes 4128768 | tf_op jit(solution)/shard_map/all_to_all | solution.py:47
  19.6 0.1 copy.14
  19.7 0.1 reduce
  19.8 0.1 convert_reduce_fusion
  19.9 0.1 select_reduce_fusion
  20.1 27.6 %all-to-all-done = bf16[56,16,1152]{2,0,1:T(8,128)(2,1)S(1)} async-done(((bf16[56,16,1152]{2,0,1:T(8,128)(2,1)}), bf16[56,16,1152]{2,0,1:T(8,128)(2,1)S(1)}, u32[]{:S(2)}, u32[]{:S(2)}) %all-to-all-start) | async-done | bytes 2064416 | tf_op jit(solution)/shard_map/all_to_all | solution.py:47
  47.6 2.3 gather_fusion
  49.9 1.1 broadcast_select_fusion
  51.2 166.8 %all-gather.4.cloned.1.call-done = bf16[3584,1152]{1,0:T(8,128)(2,1)} async-done(((bf16[448,1152]{1,0:T(8,128)(2,1)}), bf16[3584,1152]{1,0:T(8,128)(2,1)}) %all-gather.4.cloned.1.call-update) | async-done | bytes 8257552 | tf_op jit(solution)/shard_map/all_gather | solution.py:54
  218.0 11.7 %convolution_bitcast_fusion.1 = f32[3584,448]{1,0:T(8,128)} fusion(bf16[448,1152]{1,0:T(8,128)(2,1)} %broadcast_select_fusion, bf16[3584,1152]{1,0:T(8,128)(2,1)} %all-gather.4.cloned.1.call-done), kind=kOutput, calls=%fused_computation.7 | convolution fusion | flops 3699376128 | bytes 15712256
  229.7 98.5 %reduce-scatter.7.cloned.1.call-done = f32[224,448]{1,0:T(8,128)} async-done(((f32[3584,448]{1,0:T(8,128)}), f32[224,448]{1,0:T(8,128)}) %reduce-scatter.7.cloned.1.call-update) | async-done | bytes 401424
  328.2 1.2 copy.20
  329.4 0.8 broadcast_multiply_fusion
  330.3 80.0 %all-gather.6.cloned.1.call-done = f32[3584,224]{1,0:T(8,128)} async-done(((f32[448,224]{1,0:T(8,128)}), f32[3584,224]{1,0:T(8,128)}) %all-gather.6.cloned.1.call-update) | async-done | bytes 3211280 | tf_op jit(solution)/shard_map/all_gather | solution.py:57
  410.3 10.0 %convolution_bitcast_fusion = f32[3584,448]{1,0:T(8,128)} fusion(f32[3584,224]{1,0:T(8,128)} %all-gather.6.cloned.1.call-done, f32[448,224]{1,0:T(8,128)S(1)} %copy.20), kind=kOutput, calls=%fused_computation.6 | convolution fusion | flops 4316039168 | bytes 10035200
  420.4 0.2 all-gather.8.cloned.1.call-start
  420.6 94.1 %reduce-scatter.9.cloned.1.call-done = f32[224,448]{1,0:T(8,128)} async-done(((f32[3584,448]{1,0:T(8,128)}), f32[224,448]{1,0:T(8,128)}) %reduce-scatter.9.cloned.1.call-update) | async-done | bytes 401424
  514.7 1.2 copy.22
  516.0 1.0 copy.16
  517.0 0.1 min.22
  517.2 0.1 iota_compare_fusion.2
  517.3 69.1 %all-gather.8.cloned.1.call-done = f32[448,3584]{0,1:T(8,128)} async-done(((f32[448,224]{0,1:T(8,128)}), f32[448,3584]{0,1:T(8,128)}) %all-gather.8.cloned.1.call-update) | async-done | bytes 6422544 | tf_op jit(solution)/shard_map/all_gather | solution.py:69
  586.3 46.5 %while.14 = (s32[]{:T(128)}, f32[448,1152]{1,0:T(8,128)S(1)}, f32[448,3584]{0,1:T(8,128)}, bf16[3584,1152]{1,0:T(8,128)(2,1)}, s32[]{:T(128)}, /*index=5*/s32[]{:T(128)}, s32[]{:T(128)}, s32[]{:T(128)}) while((s32[]{:T(128)}, f32[448,1152]{1,0:T(8,128)S(1)}, f32[448,3584]{0,1:T(8,128)}, bf16[3584,1152]{1,0:T(8,128)(2,1)}, ...), condition=%wide.region_6.7_spmd.clone, body=%wide.region_5.6_spmd.clone.sunk | while | flops 1388298240 | bytes 5105292 | solution.py:32
  586.3 2.9 convolution_add_fusion.2
  589.2 2.9 convolution_add_fusion.2
  592.1 2.9 convolution_add_fusion.2
  595.0 2.9 convolution_add_fusion.2
  597.9 2.9 convolution_add_fusion.2
  600.9 2.9 convolution_add_fusion.2
  603.8 2.9 convolution_add_fusion.2
  606.7 2.9 convolution_add_fusion.2
  609.6 2.9 convolution_add_fusion.2
  612.5 2.9 convolution_add_fusion.2
  615.4 2.9 convolution_add_fusion.2
  618.3 2.9 convolution_add_fusion.2
  621.2 2.9 convolution_add_fusion.2
  624.1 2.9 convolution_add_fusion.2
  627.0 2.9 convolution_add_fusion.2
  629.9 2.9 convolution_add_fusion.2
  632.8 1.3 copy-done
  634.1 1.9 multiply_add_fusion
  636.0 4.3 gather_fusion.1
  640.4 2.5 select_select_fusion
  642.9 52.7 %all_to_all.32 = f32[16,56,1152]{2,1,0:T(8,128)S(1)} all-to-all(f32[16,56,1152]{2,1,0:T(8,128)S(1)} %select_select_fusion), channel_id=1, replica_groups=mesh['gr'=16,'gc'=8] {'gr'}, dimensions={0} | all-to-all | bytes 8257536 | tf_op jit(solution)/shard_map/all_to_all | solution.py:78
  695.6 2.7 copy.18
  698.3 5.0 reshape.143
  (26 shorter events, 0.5 us)
Async XLA Ops:
  8.4 11.2 %copy-start.1 = (s32[8,16]{1,0:T(8,128)S(1)}, s32[8,16]{1,0:T(8,128)}, u32[]{:S(2)}) copy-start(s32[8,16]{1,0:T(8,128)} %param.5) | copy-start | bytes 1540
  10.1 37.6 %all-to-all-start = ((bf16[56,16,1152]{2,0,1:T(8,128)(2,1)}), bf16[56,16,1152]{2,0,1:T(8,128)(2,1)S(1)}, u32[]{:S(2)}, u32[]{:S(2)}) async-start(bf16[56,16,1152]{2,0,1:T(8,128)(2,1)} %copy.15), calls=%async_computation | async-start | bytes 4128768 | tf_op jit(solution)/shard_map/all_to_all | solution.py:47
  19.5 198.5 %all-gather.4.cloned.1.call-start = ((), (), s32[]{:S(2)}) async-start(), calls=%async_computation.4 | async-start | bytes 9289728 | tf_op jit(solution)/shard_map/all_gather | solution.py:54
  51.1 277.1 %reduce-scatter.7.cloned.1.call-start = ((), (), s32[]{:S(2)}) async-start(), calls=%async_computation.7 | async-start | bytes 7798784
  229.7 180.6 %all-gather.6.cloned.1.call-start = ((), (), s32[]{:S(2)}) async-start(), calls=%async_computation.5 | async-start | bytes 4128768 | tf_op jit(solution)/shard_map/all_gather | solution.py:57
  330.3 184.4 %reduce-scatter.9.cloned.1.call-start = ((), (), s32[]{:S(2)}) async-start(), calls=%async_computation.8 | async-start | bytes 7798784
  420.4 166.0 %all-gather.8.cloned.1.call-start = ((), (), s32[]{:S(2)}) async-start(), calls=%async_computation.6 | async-start | bytes 7798784 | tf_op jit(solution)/shard_map/all_gather | solution.py:69
  632.8 1.3 copy-start
Sparse Core Ops, SparseCore 0:
  51.2 166.7 all-gather.3
  229.8 98.3 reduce-scatter.6
  330.4 79.8 all-gather.5
  420.5 94.1 reduce-scatter.8
  517.1 69.2 all-gather.7
where the time goes:
time: 711 us; the launch traced here: 710 us
  waiting for transfers between devices  536 us (75%)
  matrix products  67.7 us (10%)
  blocking collectives  52.7 us (7%)
  local copies, waits for them, and re-layouts  22.7 us (3%)
  between operations  13.3 us (2%)
  starting transfers between devices  9.85 us (1%)
    unnamed x7, waiting for transfers between devices  193 us
    all_gather x1, waiting for transfers between devices, body(): panel = lax.all_gather(own_block, 'gc', axis=0, tiled=True)  167 us
    all_gather x1, waiting for transfers between devices, body(): gram_cols = lax.all_gather(gram_block, 'gc', axis=0, tiled=True)  80 us
    all_gather x1, waiting for transfers between devices, body(): lax.all_gather(poly_block, 'gr', axis=1, tiled=True)  69.1 us
    all_to_all x1, blocking collectives, body(): lax.all_to_all(outgoing, 'gr', split_axis=0, concat_axis=1, tiled=True)  52.7 us
    dot_general x16, matrix products, one_turn(): jnp.dot(seg_part, panel_rows, precision=highest, preferred_element_type=j...  46 us
    all_to_all x1, waiting for transfers between devices, body(): lax.all_to_all(own_rows, 'gr', split_axis=1, concat_axis=0, tiled=True)  27.6 us
    unnamed x2, matrix products  21.7 us
  transfers between devices with their start and end apart: 6, of which 6 were waited for; matrix products, arithmetic and copies ran while one was open for 0% of the time, Pallas kernels for 0%

commit v1 on v0

--- a/solution.py
+++ b/solution.py
@@ -1,7 +1,9 @@
+import functools
 import jax
 import jax.numpy as jnp
 from jax import lax
 from jax.sharding import PartitionSpec as P
+from jax.lax import all_to_all, axis_size
 
 M = 3584
 N = 18432
@@ -9,6 +11,16 @@
 cubic_coef = -4.775
 quintic_coef = 2.0315
 highest = lax.Precision.HIGHEST
+
+
+def settle_panels_over_axis(patch, axis_key):
+    kept_arr = jnp.concatenate(
+        all_to_all(jnp.stack(axis_size(axis_key) * [patch]), axis_key, 0, 0), axis=0
+    )
+    return kept_arr
+
+
+columns_derive = functools.partial(settle_panels_over_axis, axis_key="gc")
 
 
 def rows_against(left_rows, right_rows):
@@ -51,7 +63,7 @@
     first_row = jnp.sum(jnp.where(one_hot, my_starts[None, :], 0), axis=1)
     source_rows = holder * capacity + position - first_row
     own_block = jnp.take(received, source_rows, axis=0)
-    panel = lax.all_gather(own_block, "gc", axis=0, tiled=True)
+    panel = columns_derive(own_block)
     partial_value = rows_against(own_block, panel)
     gram_block = lax.psum_scatter(partial_value, "gr", scatter_dimension=1, tiled=True) / N
     gram_cols = lax.all_gather(gram_block, "gc", axis=0, tiled=True)

time: 711 us -> 634 us (0.89)
  waiting for transfers between devices: 536 us -> 365 us
  blocking collectives: 52.7 us -> 148 us
    all_gather x1 -> x0, waiting for transfers between devices: 167 us -> none  [body(): panel = lax.all_gather(own_block, 'gc', axis=0, tiled=True)]
    all_to_all x0 -> x1, blocking collectives: none -> 95.6 us  [settle_panels_over_axis(): all_to_all(jnp.stack(axis_size(axis_key) * [patch]), axis_key, 0, 0)]
    unnamed x7 -> x6, waiting for transfers between devices: 193 us -> 188 us
  transfers between devices with their start and end apart: 6 -> 5, of which waited for: 6 -> 5; matrix products, arithmetic and copies ran while one was open for 0% -> 0% of each run, Pallas kernels for 0% -> 0%
where the time goes in v1:
time: 634 us; the launch traced here: 633 us
  waiting for transfers between devices  365 us (58%)
  blocking collectives  148 us (23%)
  matrix products  63.1 us (10%)
  local copies, waits for them, and re-layouts  26.9 us (4%)
  between operations  13.3 us (2%)
  starting transfers between devices  9.8 us (2%)
    unnamed x6, waiting for transfers between devices  188 us
    all_to_all x1, blocking collectives, settle_panels_over_axis(): all_to_all(jnp.stack(axis_size(axis_key) * [patch]), axis_key, 0, 0)  95.6 us
    all_gather x1, waiting for transfers between devices, body(): gram_cols = lax.all_gather(gram_block, 'gc', axis=0, tiled=True)  80.1 us
    all_gather x1, waiting for transfers between devices, body(): lax.all_gather(poly_block, 'gr', axis=1, tiled=True)  69.1 us
    all_to_all x1, blocking collectives, body(): lax.all_to_all(outgoing, 'gr', split_axis=0, concat_axis=1, tiled=True)  52.7 us
    dot_general x16, matrix products, one_turn(): jnp.dot(seg_part, panel_rows, precision=highest, preferred_element_type=j...  46 us
    all_to_all x1, waiting for transfers between devices, body(): lax.all_to_all(own_rows, 'gr', split_axis=1, concat_axis=0, tiled=True)  27.6 us
    unnamed x2, matrix products  17.1 us
  transfers between devices with their start and end apart: 5, of which 5 were waited for; matrix products, arithmetic and copies ran while one was open for 0% of the time, Pallas kernels for 0%

profile of v1, /device:TPU:1, one launch (start us, length us, event | category | flops | bytes accessed | tf_op | source)
XLA Modules:
  0.0 633.2 jit_solution(17714890843271205389)
XLA Ops:
  6.5 1.8 copy.24
  8.4 1.7 copy.15
  10.1 9.5 %all-to-all-start = ((bf16[56,16,1152]{2,0,1:T(8,128)(2,1)}), bf16[56,16,1152]{2,0,1:T(8,128)(2,1)S(1)}, u32[]{:S(2)}, u32[]{:S(2)}) async-start(bf16[56,16,1152]{2,0,1:T(8,128)(2,1)} %copy.15), calls=%async_computation | async-start | bytes 4128768 | tf_op jit(solution)/shard_map/all_to_all | solution.py:59
  19.7 0.1 reduce
  19.8 0.1 convert_reduce_fusion
  19.9 0.1 select_reduce_fusion
  20.1 27.6 %all-to-all-done = bf16[56,16,1152]{2,0,1:T(8,128)(2,1)S(1)} async-done(((bf16[56,16,1152]{2,0,1:T(8,128)(2,1)}), bf16[56,16,1152]{2,0,1:T(8,128)(2,1)S(1)}, u32[]{:S(2)}, u32[]{:S(2)}) %all-to-all-start) | async-done | bytes 2064416 | tf_op jit(solution)/shard_map/all_to_all | solution.py:59
  47.6 2.3 gather_fusion
  49.9 0.2 broadcast_select_fusion
  50.1 1.1 stack.2
  51.2 95.6 %all_to_all.37 = bf16[8,448,1152]{2,1,0:T(8,128)(2,1)S(1)} all-to-all(bf16[8,448,1152]{2,1,0:T(8,128)(2,1)S(1)} %stack.2), channel_id=1, replica_groups=mesh['gr'=16,'gc'=8] {'gc'}, dimensions={0} | all-to-all | bytes 16515072 | tf_op jit(solution)/shard_map/all_to_all | solution.py:18
  146.8 3.2 copy-done.1
  150.0 7.1 %convolution_bitcast_fusion.1 = f32[3584,448]{1,0:T(8,128)} fusion(bf16[448,1152]{1,0:T(8,128)(2,1)S(1)} %broadcast_select_fusion, bf16[3584,1152]{1,0:T(8,128)(2,1)S(1)} %bitcast.36), kind=kOutput, calls=%fused_computation.7 | convolution fusion | flops 3699376128 | bytes 15712256
  157.2 94.3 %reduce-scatter.7.cloned.1.call-done = f32[224,448]{1,0:T(8,128)} async-done(((f32[3584,448]{1,0:T(8,128)}), f32[224,448]{1,0:T(8,128)}) %reduce-scatter.7.cloned.1.call-update) | async-done | bytes 401424
  251.5 1.2 copy.20
  252.7 0.8 broadcast_multiply_fusion
  253.6 80.1 %all-gather.3.cloned.1.call-done = f32[3584,224]{1,0:T(8,128)} async-done(((f32[448,224]{1,0:T(8,128)}), f32[3584,224]{1,0:T(8,128)}) %all-gather.3.cloned.1.call-update) | async-done | bytes 3211280 | tf_op jit(solution)/shard_map/all_gather | solution.py:69
  333.7 10.0 %convolution_bitcast_fusion = f32[3584,448]{1,0:T(8,128)} fusion(f32[3584,224]{1,0:T(8,128)} %all-gather.3.cloned.1.call-done, f32[448,224]{1,0:T(8,128)S(1)} %copy.20), kind=kOutput, calls=%fused_computation.6 | convolution fusion | flops 4316039168 | bytes 10035200
  343.7 0.2 all-gather.5.cloned.1.call-start
  343.9 94.1 %reduce-scatter.9.cloned.1.call-done = f32[224,448]{1,0:T(8,128)} async-done(((f32[3584,448]{1,0:T(8,128)}), f32[224,448]{1,0:T(8,128)}) %reduce-scatter.9.cloned.1.call-update) | async-done | bytes 401424
  438.0 1.2 copy.22
  439.3 1.0 copy.16
  440.4 0.1 min.22
  440.6 69.1 %all-gather.5.cloned.1.call-done = f32[448,3584]{0,1:T(8,128)} async-done(((f32[448,224]{0,1:T(8,128)}), f32[448,3584]{0,1:T(8,128)}) %all-gather.5.cloned.1.call-update) | async-done | bytes 6422544 | tf_op jit(solution)/shard_map/all_gather | solution.py:81
  509.7 46.5 %while.14 = (s32[]{:T(128)}, f32[448,1152]{1,0:T(8,128)S(1)}, f32[448,3584]{0,1:T(8,128)}, bf16[3584,1152]{1,0:T(8,128)(2,1)}, s32[]{:T(128)}, /*index=5*/s32[]{:T(128)}, s32[]{:T(128)}, s32[]{:T(128)}) while((s32[]{:T(128)}, f32[448,1152]{1,0:T(8,128)S(1)}, f32[448,3584]{0,1:T(8,128)}, bf16[3584,1152]{1,0:T(8,128)(2,1)}, ...), condition=%wide.region_6.7_spmd.clone, body=%wide.region_5.6_spmd.clone.sunk | while | flops 1388298240 | bytes 5105292 | solution.py:44
  509.7 2.9 convolution_add_fusion.2
  512.6 2.9 convolution_add_fusion.2
  515.5 2.9 convolution_add_fusion.2
  518.4 2.9 convolution_add_fusion.2
  521.3 2.9 convolution_add_fusion.2
  524.2 2.9 convolution_add_fusion.2
  527.1 2.9 convolution_add_fusion.2
  530.0 2.9 convolution_add_fusion.2
  532.9 2.9 convolution_add_fusion.2
  535.8 2.9 convolution_add_fusion.2
  538.8 2.9 convolution_add_fusion.2
  541.7 2.9 convolution_add_fusion.2
  544.6 2.9 convolution_add_fusion.2
  547.5 2.9 convolution_add_fusion.2
  550.4 2.9 convolution_add_fusion.2
  553.3 2.9 convolution_add_fusion.2
  556.2 1.3 copy-done
  557.5 1.9 multiply_add_fusion
  559.4 4.3 gather_fusion.1
  563.7 2.5 select_select_fusion
  566.2 52.7 %all_to_all.38 = f32[16,56,1152]{2,1,0:T(8,128)S(1)} all-to-all(f32[16,56,1152]{2,1,0:T(8,128)S(1)} %select_select_fusion), channel_id=1, replica_groups=mesh['gr'=16,'gc'=8] {'gr'}, dimensions={0} | all-to-all | bytes 8257536 | tf_op jit(solution)/shard_map/all_to_all | solution.py:90
  619.0 2.7 copy.18
  621.6 5.0 reshape.154
  (27 shorter events, 0.6 us)
Async XLA Ops:
  8.4 11.2 %copy-start.2 = (s32[8,16]{1,0:T(8,128)S(1)}, s32[8,16]{1,0:T(8,128)}, u32[]{:S(2)}) copy-start(s32[8,16]{1,0:T(8,128)} %param.5) | copy-start | bytes 1540
  10.1 37.6 %all-to-all-start = ((bf16[56,16,1152]{2,0,1:T(8,128)(2,1)}), bf16[56,16,1152]{2,0,1:T(8,128)(2,1)S(1)}, u32[]{:S(2)}, u32[]{:S(2)}) async-start(bf16[56,16,1152]{2,0,1:T(8,128)(2,1)} %copy.15), calls=%async_computation | async-start | bytes 4128768 | tf_op jit(solution)/shard_map/all_to_all | solution.py:59
  19.5 232.0 %reduce-scatter.7.cloned.1.call-start = ((), (), s32[]{:S(2)}) async-start(), calls=%async_computation.7 | async-start | bytes 7798784
  146.8 3.2 copy-start.1
  157.2 176.5 %all-gather.3.cloned.1.call-start = ((), (), s32[]{:S(2)}) async-start(), calls=%async_computation.5 | async-start | bytes 4128768 | tf_op jit(solution)/shard_map/all_gather | solution.py:69
  253.6 184.5 %reduce-scatter.9.cloned.1.call-start = ((), (), s32[]{:S(2)}) async-start(), calls=%async_computation.8 | async-start | bytes 7798784
  343.7 166.0 %all-gather.5.cloned.1.call-start = ((), (), s32[]{:S(2)}) async-start(), calls=%async_computation.6 | async-start | bytes 7798784 | tf_op jit(solution)/shard_map/all_gather | solution.py:81
  556.2 1.3 copy-start
Sparse Core Ops, SparseCore 0:
  157.3 94.2 reduce-scatter.6
  253.7 79.9 all-gather.2
  343.8 94.1 reduce-scatter.8
  440.4 69.2 all-gather.4
